TPU v7x, 512 devices: a whole 4x4x16 slice. The times are simulated.
512 devices in a mesh: ctx: 64 (over x, z), head: 8 (over y, core).
Axes of the slice: x: 4, y: 4, z: 16, core: 2. Of those that a mesh axis runs over, the one named last changes fastest.
Arguments:
- hidden_in: bfloat16 [65536, 2048], P('ctx', 'head'), may hold values from -6 to 6
- proj_weight: bfloat16 [2048, 3584], P(None, 'head'), may hold values from -0.125 to 0.125
- conv_weight: float32 [3, 1024], P(None, 'head'), may hold values from -3 to 3
- norm_gain: float32 [1024], P('head'), may hold values from 0.1 to 1.9
- out_weight: bfloat16 [1024, 2048], P('head'), may hold values from -0.25 to 0.25
Outputs:
- layer_out: bfloat16 [65536, 2048], P('ctx', 'head')
All inputs are finite; a program needn't handle non-finite values.
Results may differ from a plain program's by a relative error of at most 0.014.
Values may be sent and summed in bfloat16 or wider, within the bound.
A program may use at most 64 MiB of HBM per device.

v0:
```python
import jax
import jax.numpy as jnp
from jax import lax
from jax.sharding import PartitionSpec as P

DV = 64
FQK = 16
WIN = 64
CONV = 3


def shifted(value, axis, by):
    count = lax.axis_size(axis)
    pairs = [(i, i + by) for i in range(count) if 0 <= i + by < count]
    return lax.ppermute(value, axis, pairs)


def features(vector):
    vec_len = vector.shape[-1]
    square = (vector[..., :, None] * vector[..., None, :]).reshape(
        vector.shape[:-1] + (vec_len * vec_len,)
    )
    constant = jnp.ones(vector.shape[:-1] + (1,), vector.dtype)
    return jnp.concatenate(
        [constant, vector / vec_len**0.25, square / (2.0 * vec_len) ** 0.5], axis=-1
    )


def normalize(block_in):
    values = block_in.astype(jnp.float32)
    return (values * lax.rsqrt(jnp.mean(values * values, axis=-1, keepdims=True) + 1e-06)).astype(
        jnp.bfloat16
    )


def convolve(extended, conv_weight, count):
    tap_count = conv_weight.shape[0]
    total = jnp.zeros((count, extended.shape[1]), jnp.float32)
    for tap_id in range(tap_count):
        offset = tap_count - 1 - tap_id
        total = total + conv_weight[tap_id] * extended[offset : offset + count].astype(jnp.float32)
    return total.astype(jnp.bfloat16)


def per_device(hidden_in, proj_weight, conv_weight, norm_gain, out_weight):
    highest = lax.Precision.HIGHEST
    row_count = hidden_in.shape[0]
    head_count = out_weight.shape[0] // DV
    per_head = 2 * FQK + 3 * DV
    reach_rows = WIN - 1
    edge_rows = CONV - 1
    projected = jnp.dot(
        lax.all_gather(hidden_in, "head", axis=1, tiled=True),
        proj_weight,
        preferred_element_type=jnp.float32,
    ).astype(jnp.bfloat16)
    projected = projected.reshape(row_count, head_count, per_head)
    lin_query = projected[:, :, :FQK]
    lin_key = projected[:, :, FQK : 2 * FQK]
    raw_values = projected[:, :, 2 * FQK : 2 * FQK + DV].reshape(row_count, head_count * DV)
    win_query = projected[:, :, 2 * FQK + DV : 2 * FQK + 2 * DV]
    win_key = projected[:, :, 2 * FQK + 2 * DV :].reshape(row_count, head_count * DV)
    before_rows = shifted(raw_values[row_count - edge_rows :], "ctx", 1)
    conv_values = convolve(jnp.concatenate([before_rows, raw_values], 0), conv_weight, row_count)
    prev_values, prev_keys = shifted(
        (conv_values[row_count - reach_rows :], win_key[row_count - reach_rows :]), "ctx", 1
    )
    value_grid = conv_values.reshape(row_count, head_count, DV)
    value_full = value_grid.astype(jnp.float32)
    key_feat = features(lin_key.astype(jnp.float32))
    own_state = jnp.einsum("thf,thd->fhd", key_feat, value_full, precision=highest)
    feat_count = own_state.shape[0]
    flat_state = own_state.reshape(feat_count, head_count * DV)
    position = lax.axis_index("ctx")
    piece = lax.all_gather(flat_state[None], "ctx", axis=0, tiled=True)
    shard_ids = jnp.arange(piece.shape[0], dtype=jnp.int32)
    lower_mask = (shard_ids < position)[:, None, None]
    prior = jnp.sum(jnp.where(lower_mask, piece, 0.0), axis=0)
    prior_grid = prior.reshape(feat_count, head_count, DV)
    query_feat = features(lin_query.astype(jnp.float32))
    carried = jnp.einsum("thf,fhd->thd", query_feat, prior_grid, precision=highest)
    block_rows = min(row_count, 512)
    block_total = row_count // block_rows
    key_pos = jnp.arange(row_count, dtype=jnp.int32)

    def local_block(block_id):
        offset = block_id * block_rows
        query_part = lax.dynamic_slice_in_dim(lin_query, offset, block_rows, 0)
        products = jnp.einsum(
            "thf,shf->hts", query_part, lin_key, preferred_element_type=jnp.float32
        )
        scaled = products / FQK**0.5
        query_pos = offset + jnp.arange(block_rows, dtype=jnp.int32)
        visible = key_pos[None, :] <= query_pos[:, None]
        kernel = jnp.where(visible[None], 1.0 + scaled + 0.5 * scaled * scaled, 0.0).astype(
            jnp.bfloat16
        )
        return jnp.einsum("hts,shd->thd", kernel, value_grid, preferred_element_type=jnp.float32)

    own_part = lax.map(local_block, jnp.arange(block_total, dtype=jnp.int32)).reshape(
        row_count, head_count, DV
    )
    lin = carried + own_part
    ext_keys = normalize(
        jnp.concatenate([prev_keys, win_key], 0).reshape(row_count + reach_rows, head_count, DV)
    )
    ext_values = jnp.concatenate([prev_values, conv_values], 0).reshape(
        row_count + reach_rows, head_count, DV
    )
    query_norm = normalize(win_query)
    first_token = position * row_count
    shift_ids = (
        jnp.arange(block_rows + reach_rows, dtype=jnp.int32)[None, :]
        - jnp.arange(block_rows, dtype=jnp.int32)[:, None]
    )
    band = (shift_ids >= 0) & (shift_ids <= reach_rows)

    def window_block(block_id):
        offset = block_id * block_rows
        query_part = lax.dynamic_slice_in_dim(query_norm, offset, block_rows, 0)
        key_part = lax.dynamic_slice_in_dim(ext_keys, offset, block_rows + reach_rows, 0)
        value_part = lax.dynamic_slice_in_dim(ext_values, offset, block_rows + reach_rows, 0)
        scores = (
            jnp.einsum("thd,shd->hts", query_part, key_part, preferred_element_type=jnp.float32)
            / DV**0.5
        )
        global_pos = (
            first_token + offset + jnp.arange(block_rows + reach_rows, dtype=jnp.int32) - reach_rows
        )
        allowed = band & (global_pos >= 0)[None, :]
        expo = jnp.where(allowed[None], jnp.exp(scores), 0.0)
        weights = (expo / jnp.sum(expo, axis=-1, keepdims=True)).astype(jnp.bfloat16)
        return jnp.einsum("hts,shd->thd", weights, value_part, preferred_element_type=jnp.float32)

    window = lax.map(window_block, jnp.arange(block_total, dtype=jnp.int32)).reshape(
        row_count, head_count, DV
    )
    mean_sq = jnp.mean(lin * lin, axis=-1, keepdims=True)
    gain_grid = norm_gain.reshape(head_count, DV)
    mixed_heads = (lin * lax.rsqrt(mean_sq + 1e-05) * gain_grid + window).astype(jnp.bfloat16)
    mixed_flat = mixed_heads.reshape(row_count, head_count * DV)
    partial_out = jnp.dot(mixed_flat, out_weight, preferred_element_type=jnp.float32)
    return lax.psum_scatter(
        partial_out.astype(jnp.bfloat16), "head", scatter_dimension=1, tiled=True
    )


def solution(mesh):
    return jax.shard_map(
        per_device,
        mesh=mesh,
        in_specs=(P("ctx", "head"), P(None, "head"), P(None, "head"), P("head"), P("head", None)),
        out_specs=P("ctx", "head"),
        check_vma=False,
    )
```

profile of v0, /device:TPU:1, one launch (start us, length us, event | category | flops | bytes accessed | tf_op | source)
XLA Modules:
  0.0 290.8 jit_solution(8523061620894326594)
XLA Ops:
  8.1 50.3 %all-gather.3.cloned.1.call-done = bf16[1024,2048]{1,0:T(8,128)(2,1)} async-done(((bf16[1024,256]{1,0:T(8,128)(2,1)}), bf16[1024,2048]{1,0:T(8,128)(2,1)}) %all-gather.3.cloned.1.call-update) | async-done | bytes 4194320 | tf_op jit(solution)/shard_map/all_gather | solution.py:53
  58.4 4.3 %convolution_convert_fusion.1 = bf16[1024,448]{0,1:T(8,128)(2,1)S(1)} fusion(bf16[1024,2048]{1,0:T(8,128)(2,1)} %all-gather.3.cloned.1.call-done, bf16[2048,448]{0,1:T(8,128)(2,1)S(1)} %copy-done), kind=kOutput, calls=%fused_computation.46 | convolution fusion | flops 1879506944 | bytes 6946816 | tf_op jit(solution)/shard_map/dot_general | solution.py:52
  63.5 3.2 %collective-permute-start = (bf16[2,128]{0,1:T(8,128)(2,1)S(1)}, bf16[2,128]{0,1:T(8,128)(2,1)S(1)}, u32[]{:S(2)}, u32[]{:S(2)}) collective-permute-start(bf16[2,128]{0,1:T(8,128)(2,1)S(1)} %bitcast.73), channel_id=1, source_target_pairs={{0,8},{8,16},{16,24},{24,32},{32,40},{40,48},{48,56},{56,64},{64,7... | collective-permute-start | bytes 1544 | tf_op jit(solution)/shard_map/ppermute | solution.py:15
  68.7 2.5 fusion.29
  72.9 4.2 %collective-permute-start.2 = (bf16[63,128]{0,1:T(8,128)(2,1)}, bf16[63,128]{0,1:T(8,128)(2,1)}, u32[]{:S(2)}, u32[]{:S(2)}) collective-permute-start(bf16[63,128]{0,1:T(8,128)(2,1)} %bitcast.14), channel_id=1, source_target_pairs={{0,8},{8,16},{16,24},{24,32},{32,40},{40,48},{48,56},{56,64},{64,7... | collective-permute-start | bytes 48392 | tf_op jit(solution)/shard_map/ppermute | solution.py:15
  78.0 1.6 multiply_multiply_fusion
  79.6 1.4 slice.68
  81.0 3.2 %collective-permute-start.1 = (bf16[63,128]{0,1:T(8,128)(2,1)}, bf16[63,128]{0,1:T(8,128)(2,1)}, u32[]{:S(2)}, u32[]{:S(2)}) collective-permute-start(bf16[63,128]{0,1:T(8,128)(2,1)} %slice.68), channel_id=1, source_target_pairs={{0,8},{8,16},{16,24},{24,32},{32,40},{40,48},{48,56},{56,64},{64,7... | collective-permute-start | bytes 48392 | tf_op jit(solution)/shard_map/ppermute | solution.py:15
  84.4 14.3 %while.26 = (s32[]{:T(128)}, f32[2,512,2,64]{1,0,3,2:T(2,128)S(1)}, s32[2]{0:T(128)S(1)}, bf16[1024,2,16]{0,2,1:T(8,128)(2,1)}, bf16[1024,2,16]{0,2,1:T(8,128)(2...) while((s32[]{:T(128)}, f32[2,512,2,64]{1,0,3,2:T(2,128)S(1)}, ...), condition=%wide.region_2.3_spmd.clone, body=%wide.region_1.2_spmd.clone.sunk | while | flops 175636992 | bytes 2724019 | solution.py:100
  86.0 2.7 fusion.74
  89.0 2.4 dynamic_update_slice.17
  93.1 2.7 fusion.74
  96.2 2.4 dynamic_update_slice.17
  98.6 1.2 reshape.143
  103.0 14.0 %while.27 = (s32[]{:T(128)}, f32[2,512,2,64]{1,0,3,2:T(2,128)S(1)}, s32[2]{0:T(128)S(1)}, bf16[1087,2,64]{0,2,1:T(8,128)(2,1)S(1)}, s32[]{:T(128)}, /*index=5*/b...) while((s32[]{:T(128)}, f32[2,512,2,64]{1,0,3,2:T(2,128)S(1)}, ...), condition=%wide.region_8.9_spmd.clone, body=%wide.region_6.8_spmd.clone.sunk | while | flops 156327104 | bytes 7377774 | solution.py:135
  104.6 1.9 fusion.77
  107.6 2.4 dynamic_update_slice.18
  111.6 1.9 fusion.77
  114.6 2.4 dynamic_update_slice.18
  117.5 109.2 %all-gather.5.cloned.1.call-done = f32[64,273,128]{2,1,0:T(8,128)} async-done(((f32[1,273,128]{2,1,0:T(8,128)}), f32[64,273,128]{2,1,0:T(8,128)}) %all-gather.5.cloned.1.call-update) | async-done | bytes 8945680 | tf_op jit(solution)/shard_map/all_gather | solution.py:75
  226.7 4.7 %select_reduce_fusion = f32[273,128]{1,0:T(8,128)S(1)} fusion(f32[64,273,128]{2,1,0:T(8,128)} %all-gather.5.cloned.1.call-done, pred[64]{0:T(512)(128)(4,1)S(1)} %iota_compare_fusion.1), kind=kLoop, calls=%fused_computation.32 | loop fusion | flops 4437888 | bytes 9085504 | tf_op jit(solution)/shard_map/reduce_sum | solution.py:78
  231.6 3.7 %multiply_reduce_fusion = (f32[1024,2]{0,1:T(2,128)S(1)}, f32[1024,2,64]{0,2,1:T(8,128)S(1)}) fusion(f32[1024,2,64]{0,2,1:T(8,128)S(1)} %copy-done.1, f32[273,2,64]{0,2,1:T(8,128)S(1)} %bitcast.70, f32[1024,2,256]{0,2,1:T(8,128)} %bitcast.59, f32[1024,2,16]{0,2,1:T(8,128)S(1)} %get-tuple-element.255, f32[273]{0:T(512)S(1)} %pad.7.clone), kind=kOutput, calls=%fused_computation.60 | convolution fusion | flops 430901248 | bytes 3425860 | tf_op jit(solution)/shard_map/thf,fhd->thd/dot_general | solution.py:81
  235.5 3.2 %convolution_convert_fusion = bf16[1024,2048]{1,0:T(8,128)(2,1)} fusion(bf16[1024,128]{0,1:T(8,128)(2,1)S(1)} %bitcast.68, bf16[128,2048]{1,0:T(8,128)(2,1)S(1)} %copy-done.2), kind=kOutput, calls=%fused_computation.33 | convolution fusion | flops 538968064 | bytes 4980736 | tf_op jit(solution)/shard_map/dot_general | solution.py:142
  238.7 45.6 %reduce-scatter.2.cloned.1.call-done = bf16[1024,256]{1,0:T(8,128)(2,1)} async-done(((bf16[1024,2048]{1,0:T(8,128)(2,1)}), bf16[1024,256]{1,0:T(8,128)(2,1)}) %reduce-scatter.2.cloned.1.call-update) | async-done | bytes 524304 | tf_op jit(solution)/shard_map/reduce_scatter | solution.py:143
  (62 shorter events, 17.2 us)
Async XLA Ops:
  6.5 51.9 %copy-start = (bf16[2048,448]{0,1:T(8,128)(2,1)S(1)}, bf16[2048,448]{0,1:T(8,128)(2,1)}, u32[]{:S(2)}) copy-start(bf16[2048,448]{0,1:T(8,128)(2,1)} %param.10) | copy-start | bytes 5505028
  6.5 51.9 %all-gather.3.cloned.1.call-start = ((), (), s32[]{:S(2)}) async-start(), calls=%async_computation.1 | async-start | bytes 4718592 | tf_op jit(solution)/shard_map/all_gather | solution.py:53
  7.3 219.5 %all-gather.5.cloned.1.call-start = ((), (), s32[]{:S(2)}) async-start(), calls=%async_computation.2 | async-start | bytes 9318400 | tf_op jit(solution)/shard_map/all_gather | solution.py:75
  63.5 4.2 %collective-permute-start = (bf16[2,128]{0,1:T(8,128)(2,1)S(1)}, bf16[2,128]{0,1:T(8,128)(2,1)S(1)}, u32[]{:S(2)}, u32[]{:S(2)}) collective-permute-start(bf16[2,128]{0,1:T(8,128)(2,1)S(1)} %bitcast.73), channel_id=1, source_target_pairs={{0,8},{8,16},{16,24},{24,32},{32,40},{40,48},{48,56},{56,64},{64,7... | collective-permute-start | bytes 1544 | tf_op jit(solution)/shard_map/ppermute | solution.py:15
  66.9 5.2 %copy-start.3 = (f32[128]{0:T(128)S(1)}, f32[128]{0:T(128)}, u32[]{:S(2)}) copy-start(f32[128]{0:T(128)} %param.12) | copy-start | bytes 1540
  72.1 212.2 %reduce-scatter.2.cloned.1.call-start = ((), (), s32[]{:S(2)}) async-start(), calls=%async_computation.3 | async-start | bytes 4718592 | tf_op jit(solution)/shard_map/reduce_scatter | solution.py:143
  72.9 27.0 %collective-permute-start.2 = (bf16[63,128]{0,1:T(8,128)(2,1)}, bf16[63,128]{0,1:T(8,128)(2,1)}, u32[]{:S(2)}, u32[]{:S(2)}) collective-permute-start(bf16[63,128]{0,1:T(8,128)(2,1)} %bitcast.14), channel_id=1, source_target_pairs={{0,8},{8,16},{16,24},{24,32},{32,40},{40,48},{48,56},{56,64},{64,7... | collective-permute-start | bytes 48392 | tf_op jit(solution)/shard_map/ppermute | solution.py:15
  81.0 20.7 %collective-permute-start.1 = (bf16[63,128]{0,1:T(8,128)(2,1)}, bf16[63,128]{0,1:T(8,128)(2,1)}, u32[]{:S(2)}, u32[]{:S(2)}) collective-permute-start(bf16[63,128]{0,1:T(8,128)(2,1)} %slice.68), channel_id=1, source_target_pairs={{0,8},{8,16},{16,24},{24,32},{32,40},{40,48},{48,56},{56,64},{64,7... | collective-permute-start | bytes 48392 | tf_op jit(solution)/shard_map/ppermute | solution.py:15
  117.5 114.1 %copy-start.1 = (f32[1024,2,64]{0,2,1:T(8,128)S(1)}, f32[1024,2,64]{0,2,1:T(8,128)}, u32[]{:S(2)}) copy-start(f32[1024,2,64]{0,2,1:T(8,128)} %reshape.143) | copy-start | bytes 1572868
  231.6 3.9 %copy-start.2 = (bf16[128,2048]{1,0:T(8,128)(2,1)S(1)}, bf16[128,2048]{1,0:T(8,128)(2,1)}, u32[]{:S(2)}) copy-start(bf16[128,2048]{1,0:T(8,128)(2,1)} %param.13) | copy-start | bytes 1572868
Sparse Core Ops, SparseCore 0:
  9.4 48.9 all-gather.2
  72.2 154.5 all-gather.4
  238.8 45.4 reduce-scatter.1
where the time goes:
time: 293 us; the launch traced here: 291 us
  waiting for transfers between devices  207 us (71%)
  matrix products  24.6 us (8%)
  local copies, waits for them, and re-layouts  19.4 us (7%)
  other arithmetic  13.4 us (5%)
  between operations  13.3 us (5%)
  starting transfers between devices  10.7 us (4%)
    all_gather x1, waiting for transfers between devices, per_device(): piece = lax.all_gather(flat_state[None], 'ctx', axis=0, tiled=True)  109 us
    all_gather x1, waiting for transfers between devices, per_device(): lax.all_gather(hidden_in, 'head', axis=1, tiled=True)  50.3 us
    reduce_scatter x1, waiting for transfers between devices, per_device(): lax.psum_scatter(partial_out.astype(jnp.bfloat16), 'head', scatter_dimens...  45.6 us
    dynamic_update_slice x8, local copies, waits for them, and re-layouts, per_device(): lax.map(local_block, jnp.arange(block_total, dtype=jnp.int32))  10.9 us
    ppermute x3, starting transfers between devices, shifted(): return lax.ppermute(value, axis, pairs)  10.6 us
  transfers between devices with their start and end apart: 6, of which 4 were waited for; matrix products, arithmetic and copies ran while one was open for 12% of the time, Pallas kernels for 0%

commit v1 on v0

v1 whole, which is shorter than its diff:
```python
import functools

import jax
import jax.numpy as jnp
import numpy as np
from jax import lax
from jax.experimental import pallas as pl
from jax.experimental.pallas import tpu as pltpu
from jax.sharding import PartitionSpec as P

DV = 64
FQK = 16
WIN = 64
CONV = 3
NZ = 16
HALO = 80
FEAT = 160
MESH = pl.DeviceIdType.MESH
F32 = jnp.float32
BF16 = jnp.bfloat16
NT = (((1,), (1,)), ((), ()))


def feature_tables():
    first = np.zeros((FEAT, FQK), np.float32)
    second = np.zeros((FEAT, FQK), np.float32)
    coef = np.zeros((3, FEAT), np.float32)
    row = 0
    for i in range(FQK):
        for j in range(i, FQK):
            first[row, i] = 1.0
            second[row, j] = 1.0
            coef[0, row] = (1.0 if i == j else 2.0**0.5) / (2.0 * FQK) ** 0.5
            row += 1
    for i in range(FQK):
        first[row, i] = 1.0
        coef[0, row] = 1.0 / FQK**0.25
        coef[1, row] = 1.0
        row += 1
    coef[2, row] = 1.0
    return np.stack([first, second]), coef


def dot(a, b):
    return jnp.dot(a, b, preferred_element_type=F32)


def dot_nt(a, b):
    return lax.dot_general(a, b, NT, preferred_element_type=F32)


def gather_matmul_kernel(x_ref, w_hbm, o_ref, buf, wv, acc, wsem, ssem, rsem):
    ctx = lax.axis_index("ctx")
    me = lax.axis_index("head")
    rows, depth = x_ref.shape
    half = rows // 2
    y = lax.div(me, 2)
    core = lax.rem(me, 2)
    other = 1 - core
    y_left, y_right, y_far = lax.rem(y + 3, 4), lax.rem(y + 1, 4), lax.rem(y + 2, 4)
    left, right = y_left * 2 + core, y_right * 2 + core
    partner = y * 2 + other
    owners = [
        left,
        right,
        y_far * 2 + core,
        partner,
        y_left * 2 + other,
        y_right * 2 + other,
        y_far * 2 + other,
    ]

    w_copy = pltpu.make_async_copy(w_hbm, wv, wsem)
    w_copy.start()
    barrier = pltpu.get_barrier_semaphore()
    for dev in (left, right, partner):
        pl.semaphore_signal(barrier, inc=1, device_id=(ctx, dev), device_id_type=MESH)
    pl.semaphore_wait(barrier, 3)

    sent = []

    def send(src, slot, part, dev):
        span = pl.ds(part * half, half)
        copy = pltpu.make_async_remote_copy(
            src_ref=src.at[span],
            dst_ref=buf.at[slot, span],
            send_sem=ssem.at[len(sent)],
            recv_sem=rsem.at[slot * 2 + part],
            device_id=(ctx, dev),
            device_id_type=MESH,
        )
        copy.start()
        sent.append(copy)

    def arrived(slot, part):
        span = pl.ds(part * half, half)
        pltpu.make_async_remote_copy(
            src_ref=buf.at[slot, span],
            dst_ref=buf.at[slot, span],
            send_sem=ssem.at[0],
            recv_sem=rsem.at[slot * 2 + part],
            device_id=(ctx, partner),
            device_id_type=MESH,
        ).wait_recv()

    def multiply(src, owner, part, mode="add"):
        w_rows = pl.ds(pl.multiple_of(owner * depth, depth), depth)
        tile = min(256, half)

        def step(i, carry):
            span = pl.ds(pl.multiple_of(part * half + i * tile, tile), tile)
            term = dot(src[span, :], wv[w_rows, :])
            if mode == "first":
                acc[span, :] = term
            elif mode == "last":
                o_ref[span, :] = (acc[span, :] + term).astype(o_ref.dtype)
            else:
                acc[span, :] += term
            return carry

        lax.fori_loop(0, half // tile, step, 0)

    send(x_ref, 0, 0, right)
    send(x_ref, 1, 1, left)
    send(x_ref, 3, 0, partner)
    send(x_ref, 3, 1, partner)
    send(x_ref, 0, 1, right)
    send(x_ref, 1, 0, left)
    w_copy.wait()
    multiply(x_ref, me, 0, "first")
    multiply(x_ref, me, 1, "first")
    for part in (0, 1):
        arrived(3, part)
        multiply(buf.at[3], owners[3], part)
    arrived(0, 0)
    send(buf.at[0], 2, 0, right)
    send(buf.at[0], 4, 0, partner)
    arrived(1, 1)
    send(buf.at[1], 2, 1, left)
    send(buf.at[1], 5, 1, partner)
    multiply(buf.at[0], owners[0], 0)
    multiply(buf.at[1], owners[1], 1)
    arrived(4, 0)
    multiply(buf.at[4], owners[4], 0)
    arrived(5, 1)
    multiply(buf.at[5], owners[5], 1)
    arrived(0, 1)
    send(buf.at[0], 4, 1, partner)
    arrived(1, 0)
    send(buf.at[1], 5, 0, partner)
    multiply(buf.at[0], owners[0], 1)
    multiply(buf.at[1], owners[1], 0)
    arrived(4, 1)
    multiply(buf.at[4], owners[4], 1)
    arrived(5, 0)
    multiply(buf.at[5], owners[5], 0)
    arrived(2, 0)
    send(buf.at[2], 6, 0, partner)
    arrived(2, 1)
    send(buf.at[2], 6, 1, partner)
    multiply(buf.at[2], owners[2], 0)
    multiply(buf.at[2], owners[2], 1)
    for part in (0, 1):
        arrived(6, part)
        multiply(buf.at[6], owners[6], part, "last")
    for copy in sent:
        copy.wait_send()


def gather_matmul(x, w, name, collective_id):
    rows, depth = x.shape
    cols = w.shape[1]
    return pl.pallas_call(
        gather_matmul_kernel,
        out_shape=jax.ShapeDtypeStruct((rows, cols), BF16),
        in_specs=[pl.BlockSpec(memory_space=pltpu.VMEM), pl.BlockSpec(memory_space=pl.ANY)],
        out_specs=pl.BlockSpec(memory_space=pltpu.VMEM),
        scratch_shapes=[
            pltpu.VMEM((7, rows, depth), BF16),
            pltpu.VMEM(w.shape, BF16),
            pltpu.VMEM((rows, cols), F32),
            pltpu.SemaphoreType.DMA,
            pltpu.SemaphoreType.DMA((14,)),
            pltpu.SemaphoreType.DMA((14,)),
        ],
        compiler_params=pltpu.CompilerParams(
            collective_id=collective_id, has_side_effects=True, vmem_limit_bytes=48 << 20
        ),
        name=name,
    )(x, w)


def rms_unit(values, eps):
    return values * lax.rsqrt(jnp.mean(values * values, axis=-1, keepdims=True) + eps)


def mix_kernel(
    nz,
    nx,
    p_ref,
    cw_ref,
    gain_ref,
    wo_ref,
    sel_ref,
    col_ref,
    row_ref,
    m_ref,
    wcol_ref,
    halo,
    raw,
    cv,
    kh,
    qh,
    fk,
    fq,
    own,
    win,
    mine,
    zbuf,
    tot,
    xbuf,
    pre,
    wcs,
    hsem,
    zsend,
    zrecv,
    xsend,
    xrecv,
    wsend,
    wrecv,
    wloc,
):
    ctx = lax.axis_index("ctx")
    me = lax.axis_index("head")
    n_ctx = nz * nx
    n_head = 8
    rows = p_ref.shape[0]
    per_head = 2 * FQK + 3 * DV
    out_rows = wo_ref.shape[0]
    out_cols = wo_ref.shape[1] // n_head
    x = lax.div(ctx, nz)
    z = lax.rem(ctx, nz)
    after, before = lax.rem(ctx + 1, n_ctx), lax.rem(ctx + n_ctx - 1, n_ctx)

    def z_peer(d):
        return (x * nz + lax.rem(z + d, nz), me)

    def x_peer(d):
        return (lax.rem(x + d, nx) * nz + z, me)

    barrier = pltpu.get_barrier_semaphore()

    def greet(dev):
        pl.semaphore_signal(barrier, inc=1, device_id=dev, device_id_type=MESH)

    greet((after, me))
    greet((before, me))

    @pl.loop(1, nz)
    def _(d):
        greet(z_peer(d))

    for d in range(1, nx):
        greet(x_peer(d))
    for d in range(1, n_head):
        greet((ctx, lax.rem(me + d, n_head)))
    pl.semaphore_wait(barrier, 2 + (nz - 1) + (nx - 1) + (n_head - 1))

    halo_copy = pltpu.make_async_remote_copy(
        src_ref=p_ref.at[pl.ds(rows - HALO, HALO)],
        dst_ref=halo,
        send_sem=hsem.at[0],
        recv_sem=hsem.at[1],
        device_id=(after, me),
        device_id_type=MESH,
    )
    halo_copy.start()

    def weight_copy(d):
        dev = lax.rem(me + d, n_head)
        return pltpu.make_async_remote_copy(
            src_ref=wo_ref.at[:, pl.ds(pl.multiple_of(dev * out_cols, out_cols), out_cols)],
            dst_ref=wcs.at[pl.ds(pl.multiple_of(me * out_rows, out_rows), out_rows)],
            send_sem=wsend.at[d],
            recv_sem=wrecv.at[d],
            device_id=(ctx, dev),
            device_id_type=MESH,
        )

    own_weight = pltpu.make_async_copy(
        wo_ref.at[:, pl.ds(pl.multiple_of(me * out_cols, out_cols), out_cols)],
        wcs.at[pl.ds(pl.multiple_of(me * out_rows, out_rows), out_rows)],
        wloc,
    )
    own_weight.start()
    for d in range(1, n_head):
        weight_copy(d).start()

    for h in range(2):
        base = h * per_head
        lanes = slice(h * DV, (h + 1) * DV)
        key = p_ref[:, base + FQK : base + 2 * FQK]
        a = dot_nt(sel_ref[0], key)
        b = dot_nt(sel_ref[1], key)
        fk[h] = (col_ref[:, 0:1] * a * (b + col_ref[:, 1:2]) + col_ref[:, 2:3]).astype(BF16)
        at = base + 2 * FQK
        raw[HALO:, lanes] = p_ref[:, at : at + DV].astype(F32)

    halo_copy.wait()
    for h in range(2):
        at = h * per_head + 2 * FQK
        lanes = slice(h * DV, (h + 1) * DV)
        raw[:HALO, lanes] = jnp.where(ctx > 0, halo[:, at : at + DV].astype(F32), 0.0)
    n_ext = rows + WIN
    lead = HALO - WIN
    total = cw_ref[0:1, :] * raw[lead : lead + n_ext, :]
    for j in range(1, CONV):
        total = total + cw_ref[j : j + 1, :] * raw[lead - j : lead - j + n_ext, :]
    cv[...] = total.astype(BF16)

    for h in range(2):
        lanes = slice(h * DV, (h + 1) * DV)
        mine[:, lanes] = dot(fk[h], cv[WIN:, lanes]).astype(BF16)

    def z_copy(d):
        return pltpu.make_async_remote_copy(
            src_ref=mine,
            dst_ref=zbuf.at[d],
            send_sem=zsend.at[d],
            recv_sem=zrecv.at[d],
            device_id=z_peer(d),
            device_id_type=MESH,
        )

    @pl.loop(1, nz)
    def _(d):
        z_copy(d).start()

    for h in range(2):
        base = h * per_head
        lanes = slice(h * DV, (h + 1) * DV)
        at = base + 2 * FQK + DV
        qh[:, lanes] = rms_unit(p_ref[:, at : at + DV].astype(F32), 1e-6).astype(BF16)
        at = at + DV
        kh[WIN:, lanes] = rms_unit(p_ref[:, at : at + DV].astype(F32), 1e-6).astype(BF16)
        kh[:WIN, lanes] = rms_unit(halo[lead:, at : at + DV].astype(F32), 1e-6).astype(BF16)

    wb = 128
    r_id = lax.broadcasted_iota(jnp.int32, (wb, wb + WIN), 0)
    c_id = lax.broadcasted_iota(jnp.int32, (wb, wb + WIN), 1)
    band = (c_id > r_id) & (c_id <= r_id + WIN)

    def window_block(i, carry):
        start = pl.multiple_of(i * wb, wb)
        valid = band & (ctx * rows + start - WIN + c_id >= 0)
        for h in range(2):
            lanes = slice(h * DV, (h + 1) * DV)
            scores = dot_nt(qh[pl.ds(start, wb), lanes], kh[pl.ds(start, wb + WIN), lanes])
            expo = jnp.where(valid, jnp.exp(scores * (1.0 / DV**0.5)), 0.0)
            weights = (expo * (1.0 / jnp.sum(expo, axis=-1, keepdims=True))).astype(BF16)
            win[pl.ds(start, wb), lanes] = dot(weights, cv[pl.ds(start, wb + WIN), lanes])
        return carry

    lax.fori_loop(0, rows // wb, window_block, 0)

    qb = min(256, rows)
    below = lax.broadcasted_iota(jnp.int32, (qb, qb), 1) <= lax.broadcasted_iota(
        jnp.int32, (qb, qb), 0
    )

    def local_linear(h):
        base = h * per_head
        lanes = slice(h * DV, (h + 1) * DV)
        for i in range(rows // qb):
            query = p_ref[i * qb : (i + 1) * qb, base : base + FQK]
            result = None
            for s0, s1 in ((0, i * qb), (i * qb, (i + 1) * qb)):
                if s1 == s0:
                    continue
                u = dot_nt(query, p_ref[s0:s1, base + FQK : base + 2 * FQK]) * (1.0 / FQK**0.5)
                kern = 1.0 + u + 0.5 * u * u
                if s0 == i * qb:
                    kern = jnp.where(below, kern, 0.0)
                term = dot(kern.astype(BF16), cv[WIN + s0 : WIN + s1, lanes])
                result = term if result is None else result + term
            own[i * qb : (i + 1) * qb, lanes] = result

    local_linear(0)

    pre[...] = jnp.zeros_like(pre)
    pre2 = mine[...].astype(F32)

    def z_step(d, total):
        z_copy(d).wait_recv()
        part = zbuf[d].astype(F32)
        pre[...] += jnp.where(d <= z, part, 0.0)
        return total + part

    plane = lax.fori_loop(1, nz, z_step, pre2)
    tot[...] = plane.astype(BF16)

    def x_copy(d):
        return pltpu.make_async_remote_copy(
            src_ref=tot,
            dst_ref=xbuf.at[d],
            send_sem=xsend.at[d],
            recv_sem=xrecv.at[d],
            device_id=x_peer(d),
            device_id_type=MESH,
        )

    for d in range(1, nx):
        x_copy(d).start()

    for h in range(2):
        base = h * per_head
        query = p_ref[:, base : base + FQK]
        a = dot_nt(query, sel_ref[0])
        b = dot_nt(query, sel_ref[1])
        fq[h] = (row_ref[0:1, :] * a * (b + row_ref[1:2, :]) + row_ref[2:3, :]).astype(BF16)
    local_linear(1)

    for d in range(1, nx):
        x_copy(d).wait_recv()
        pre[...] += jnp.where(d <= x, xbuf[d].astype(F32), 0.0)

    for h in range(2):
        lanes = slice(h * DV, (h + 1) * DV)
        lin = own[:, lanes] + dot(fq[h], pre[:, lanes].astype(BF16))
        unit = rms_unit(lin, 1e-5)
        m_ref[:, lanes] = (unit * gain_ref[:, lanes] + win[:, lanes]).astype(BF16)

    own_weight.wait()
    for d in range(1, n_head):
        weight_copy(d).wait()
    wcol_ref[...] = wcs[...]

    @pl.loop(1, nz)
    def _(d):
        z_copy(d).wait_send()

    for d in range(1, nx):
        x_copy(d).wait_send()


def per_device(hidden_in, proj_weight, conv_weight, norm_gain, out_weight):
    rows = hidden_in.shape[0]
    n_ctx = lax.axis_size("ctx")
    nz = NZ
    nx = n_ctx // nz
    width = conv_weight.shape[1]
    n_head = lax.axis_size("head")
    out_rows = out_weight.shape[0]
    out_cols = out_weight.shape[1] // n_head
    sel, coef = feature_tables()
    projected = gather_matmul(hidden_in, proj_weight, "gather_project", 0)
    vmem = pl.BlockSpec(memory_space=pltpu.VMEM)
    dma = pltpu.SemaphoreType.DMA
    mixed, out_cols_weight = pl.pallas_call(
        functools.partial(mix_kernel, nz, nx),
        out_shape=(
            jax.ShapeDtypeStruct((rows, width), BF16),
            jax.ShapeDtypeStruct((out_rows * n_head, out_cols), BF16),
        ),
        in_specs=[vmem] * 7,
        out_specs=(vmem, vmem),
        scratch_shapes=[
            pltpu.VMEM((HALO, projected.shape[1]), BF16),
            pltpu.VMEM((rows + HALO, width), F32),
            pltpu.VMEM((rows + WIN, width), BF16),
            pltpu.VMEM((rows + WIN, width), BF16),
            pltpu.VMEM((rows, width), BF16),
            pltpu.VMEM((2, FEAT, rows), BF16),
            pltpu.VMEM((2, rows, FEAT), BF16),
            pltpu.VMEM((rows, width), F32),
            pltpu.VMEM((rows, width), F32),
            pltpu.VMEM((FEAT, width), BF16),
            pltpu.VMEM((nz, FEAT, width), BF16),
            pltpu.VMEM((FEAT, width), BF16),
            pltpu.VMEM((nx, FEAT, width), BF16),
            pltpu.VMEM((FEAT, width), F32),
            pltpu.VMEM((out_rows * n_head, out_cols), BF16),
            dma((2,)),
            dma((nz,)),
            dma((nz,)),
            dma((nx,)),
            dma((nx,)),
            dma((n_head,)),
            dma((n_head,)),
            dma,
        ],
        compiler_params=pltpu.CompilerParams(
            collective_id=1, has_side_effects=True, vmem_limit_bytes=56 << 20
        ),
        name="mix",
    )(
        projected,
        conv_weight,
        norm_gain.reshape(1, width),
        out_weight,
        jnp.asarray(sel, BF16),
        jnp.asarray(coef.T),
        jnp.asarray(coef),
    )
    return gather_matmul(mixed, out_cols_weight, "gather_out", 2)


def solution(mesh):
    return jax.shard_map(
        per_device,
        mesh=mesh,
        in_specs=(P("ctx", "head"), P(None, "head"), P(None, "head"), P("head"), P("head", None)),
        out_specs=P("ctx", "head"),
        check_vma=False,
    )
```

time: 293 us -> 109 us (0.37)
  waiting for transfers between devices: 207 us -> 0 us
  Pallas kernels: 0 us -> 102 us
  matrix products: 24.6 us -> 0 us
  other arithmetic: 13.4 us -> 0 us
  between operations: 13.3 us -> 0.06 us
  local copies, waits for them, and re-layouts: 19.4 us -> 6.6 us
  starting transfers between devices: 10.7 us -> 0 us
    all_gather x2 -> x0, waiting for transfers between devices: 160 us -> none  [the longest x1 109 us: per_device(): piece = lax.all_gather(flat_state[None], 'ctx', axis=0, tiled=True)]
    pallas_call x0 -> x3, Pallas kernels: none -> 102 us  [the longest x1 58.1 us: per_device(): pl.pallas_call(functools.partial(mix_kernel, nz, nx), out_shape=(jax.Shap...]
    reduce_scatter x1 -> x0, waiting for transfers between devices: 45.6 us -> none  [per_device(): lax.psum_scatter(partial_out.astype(jnp.bfloat16), 'head', scatter_dimens...]
    dot_general x10 -> x0, matrix products: 24.6 us -> none  [the longest x2 5.49 us: local_block(): jnp.einsum('hts,shd->thd', kernel, value_grid, preferred_element_type=jnp...]
    dynamic_update_slice x8 -> x0, local copies, waits for them, and re-layouts: 10.9 us -> none  [per_device(): lax.map(local_block, jnp.arange(block_total, dtype=jnp.int32))]
    ppermute x3 -> x0, starting transfers between devices: 10.6 us -> none  [shifted(): return lax.ppermute(value, axis, pairs)]
    unnamed x8 -> x10, local copies, waits for them, and re-layouts: 0.02 us -> 6.6 us
    reduce_sum x3 -> x0, other arithmetic: 5.67 us -> none  [the longest x1 4.67 us: per_device(): prior = jnp.sum(jnp.where(lower_mask, piece, 0.0), axis=0)]
  transfers between devices with their start and end apart: 6 -> 0, of which waited for: 4 -> 0; matrix products, arithmetic and copies ran while one was open for 12% -> 0% of each run, Pallas kernels for 0% -> 0%
where the time goes in v1:
time: 109 us
  Pallas kernels  102 us (94%)
  local copies, waits for them, and re-layouts  6.6 us (6%)
    pallas_call x1, Pallas kernels, per_device(): pl.pallas_call(functools.partial(mix_kernel, nz, nx), out_shape=(jax.Shap...  58.1 us
    pallas_call x2, Pallas kernels, gather_matmul(): pl.pallas_call(gather_matmul_kernel, out_shape=jax.ShapeDtypeStruct((rows...  44.2 us
    unnamed x10, local copies, waits for them, and re-layouts  6.6 us

profile of v1, /device:TPU:1, one launch (start us, length us, event | category | flops | bytes accessed | tf_op | source)
XLA Modules:
  0.0 109.0 jit_solution(17410911555489631889)
XLA Ops:
  0.0 0.0 copy-start.1
  0.0 2.9 %copy.9.w_hbm = bf16[2048,448]{1,0:T(8,128)(2,1)S(1)} copy(bf16[2048,448]{0,1:T(8,128)(2,1)} %param.9) | data formatting | bytes 3670016 | tf_op args[1]
  2.9 0.0 copy-done.1
  2.9 25.9 %gather_project.1.p_ref = bf16[1024,448]{1,0:T(8,128)(2,1)S(1)} custom-call(bf16[1024,256]{1,0:T(8,128)(2,1)S(1)} %copy-done.1, bf16[2048,448]{1,0:T(8,128)(2,1)S(1)} %copy.9.w_hbm), custom_call_target="tpu_custom_call" | custom-call | tf_op jit(solution)/shard_map/gather_project/pallas_call | solution.py:173
  28.8 0.0 copy-start
  28.8 1.0 copy-done
  29.8 58.1 %mix.1 = (bf16[1024,128]{1,0:T(8,128)(2,1)}, bf16[1024,256]{1,0:T(8,128)(2,1)}) custom-call(bf16[1024,448]{1,0:T(8,128)(2,1)} %copy-done, f32[3,128]{1,0:T(4,128)} %cw_ref.1, f32[1,128]{1,0:T(1,128)} %bitcast.1, bf16[128,2048]{1,0:T(8,128)(2,1)} %wo_ref.1, bf16[2,160,16]{2,1,0:T(8,128)(2,1)} %constant.6.clone.sel_ref, f32[160,3]{1,0:T(8,128)} %constant.7.clone.col_ref, ...), custom_call_target="tpu_custom_call" | custom-call | tf_op jit(solution)/shard_map/mix/pallas_call | solution.py:459
  87.9 0.0 copy-start.2
  87.9 1.0 copy-done.2
  89.0 0.0 copy-start.3
  89.0 0.9 copy-done.3
  89.9 18.3 %gather_out.1 = bf16[1024,256]{1,0:T(8,128)(2,1)S(1)} custom-call(bf16[1024,128]{1,0:T(8,128)(2,1)S(1)} %copy-done.3, bf16[1024,256]{1,0:T(8,128)(2,1)S(1)} %copy-done.2), custom_call_target="tpu_custom_call" | custom-call | tf_op jit(solution)/shard_map/gather_out/pallas_call | solution.py:173
  108.2 0.8 copy.11
Async XLA Ops:
  0.0 2.9 %copy-start.1 = (bf16[1024,256]{1,0:T(8,128)(2,1)S(1)}, bf16[1024,256]{1,0:T(8,128)(2,1)}, u32[]{:S(2)}) copy-start(bf16[1024,256]{1,0:T(8,128)(2,1)} %x_ref.1) | copy-start | bytes 1572868
  28.8 1.0 copy-start
  87.9 1.0 copy-start.2
  89.0 0.9 copy-start.3

commit v2 on v1

--- a/solution.py
+++ b/solution.py
@@ -15,6 +15,8 @@
 NZ = 16
 HALO = 80
 FEAT = 160
+SLICE = 16
+OWNER_Z = tuple(s * 8 // 5 for s in range(FEAT // SLICE))
 MESH = pl.DeviceIdType.MESH
 F32 = jnp.float32
 BF16 = jnp.bfloat16
@@ -49,11 +51,12 @@
     return lax.dot_general(a, b, NT, preferred_element_type=F32)
 
 
-def gather_matmul_kernel(x_ref, w_hbm, o_ref, buf, wv, acc, wsem, ssem, rsem):
-    ctx = lax.axis_index("ctx")
-    me = lax.axis_index("head")
-    rows, depth = x_ref.shape
-    half = rows // 2
+def rms_unit(values, eps):
+    return values * lax.rsqrt(jnp.mean(values * values, axis=-1, keepdims=True) + eps)
+
+
+def ring_gather(x_ref, buf, ctx, me, multiply, ssem, rsem, after_start):
+    half = x_ref.shape[0] // 2
     y = lax.div(me, 2)
     core = lax.rem(me, 2)
     other = 1 - core
@@ -69,14 +72,6 @@
         y_right * 2 + other,
         y_far * 2 + other,
     ]
-
-    w_copy = pltpu.make_async_copy(w_hbm, wv, wsem)
-    w_copy.start()
-    barrier = pltpu.get_barrier_semaphore()
-    for dev in (left, right, partner):
-        pl.semaphore_signal(barrier, inc=1, device_id=(ctx, dev), device_id_type=MESH)
-    pl.semaphore_wait(barrier, 3)
-
     sent = []
 
     def send(src, slot, part, dev):
@@ -103,13 +98,60 @@
             device_id_type=MESH,
         ).wait_recv()
 
+    def use(slot, part, mode="add"):
+        multiply(buf.at[slot], owners[slot], part, mode)
+
+    send(x_ref, 0, 0, right)
+    send(x_ref, 1, 1, left)
+    send(x_ref, 3, 0, partner)
+    send(x_ref, 3, 1, partner)
+    send(x_ref, 0, 1, right)
+    send(x_ref, 1, 0, left)
+    after_start()
+    for part in (0, 1):
+        arrived(3, part)
+        use(3, part)
+    arrived(0, 0)
+    send(buf.at[0], 2, 0, right)
+    send(buf.at[0], 4, 0, partner)
+    arrived(1, 1)
+    send(buf.at[1], 2, 1, left)
+    send(buf.at[1], 5, 1, partner)
+    use(0, 0)
+    use(1, 1)
+    arrived(4, 0)
+    use(4, 0)
+    arrived(5, 1)
+    use(5, 1)
+    arrived(0, 1)
+    send(buf.at[0], 4, 1, partner)
+    arrived(1, 0)
+    send(buf.at[1], 5, 0, partner)
+    use(0, 1)
+    use(1, 0)
+    arrived(4, 1)
+    use(4, 1)
+    arrived(5, 0)
+    use(5, 0)
+    arrived(2, 0)
+    send(buf.at[2], 6, 0, partner)
+    arrived(2, 1)
+    send(buf.at[2], 6, 1, partner)
+    use(2, 1)
+    use(2, 0)
+    for part in (1, 0):
+        arrived(6, part)
+        use(6, part, "last")
+    return sent
+
+
+def make_multiply(acc, o_ref, half, product):
+    tile = min(256, half)
+
     def multiply(src, owner, part, mode="add"):
-        w_rows = pl.ds(pl.multiple_of(owner * depth, depth), depth)
-        tile = min(256, half)
-
         def step(i, carry):
             span = pl.ds(pl.multiple_of(part * half + i * tile, tile), tile)
-            term = dot(src[span, :], wv[w_rows, :])
+            term = product(src[span, :], owner)
             if mode == "first":
                 acc[span, :] = term
             elif mode == "last":
@@ -120,92 +162,25 @@
 
         lax.fori_loop(0, half // tile, step, 0)
 
-    send(x_ref, 0, 0, right)
-    send(x_ref, 1, 1, left)
-    send(x_ref, 3, 0, partner)
-    send(x_ref, 3, 1, partner)
-    send(x_ref, 0, 1, right)
-    send(x_ref, 1, 0, left)
-    w_copy.wait()
-    multiply(x_ref, me, 0, "first")
-    multiply(x_ref, me, 1, "first")
-    for part in (0, 1):
-        arrived(3, part)
-        multiply(buf.at[3], owners[3], part)
-    arrived(0, 0)
-    send(buf.at[0], 2, 0, right)
-    send(buf.at[0], 4, 0, partner)
-    arrived(1, 1)
-    send(buf.at[1], 2, 1, left)
-    send(buf.at[1], 5, 1, partner)
-    multiply(buf.at[0], owners[0], 0)
-    multiply(buf.at[1], owners[1], 1)
-    arrived(4, 0)
-    multiply(buf.at[4], owners[4], 0)
-    arrived(5, 1)
-    multiply(buf.at[5], owners[5], 1)
-    arrived(0, 1)
-    send(buf.at[0], 4, 1, partner)
-    arrived(1, 0)
-    send(buf.at[1], 5, 0, partner)
-    multiply(buf.at[0], owners[0], 1)
-    multiply(buf.at[1], owners[1], 0)
-    arrived(4, 1)
-    multiply(buf.at[4], owners[4], 1)
-    arrived(5, 0)
-    multiply(buf.at[5], owners[5], 0)
-    arrived(2, 0)
-    send(buf.at[2], 6, 0, partner)
-    arrived(2, 1)
-    send(buf.at[2], 6, 1, partner)
-    multiply(buf.at[2], owners[2], 0)
-    multiply(buf.at[2], owners[2], 1)
-    for part in (0, 1):
-        arrived(6, part)
-        multiply(buf.at[6], owners[6], part, "last")
-    for copy in sent:
-        copy.wait_send()
-
-
-def gather_matmul(x, w, name, collective_id):
-    rows, depth = x.shape
-    cols = w.shape[1]
-    return pl.pallas_call(
-        gather_matmul_kernel,
-        out_shape=jax.ShapeDtypeStruct((rows, cols), BF16),
-        in_specs=[pl.BlockSpec(memory_space=pltpu.VMEM), pl.BlockSpec(memory_space=pl.ANY)],
-        out_specs=pl.BlockSpec(memory_space=pltpu.VMEM),
-        scratch_shapes=[
-            pltpu.VMEM((7, rows, depth), BF16),
-            pltpu.VMEM(w.shape, BF16),
-            pltpu.VMEM((rows, cols), F32),
-            pltpu.SemaphoreType.DMA,
-            pltpu.SemaphoreType.DMA((14,)),
-            pltpu.SemaphoreType.DMA((14,)),
-        ],
-        compiler_params=pltpu.CompilerParams(
-            collective_id=collective_id, has_side_effects=True, vmem_limit_bytes=48 << 20
-        ),
-        name=name,
-    )(x, w)
-
-
-def rms_unit(values, eps):
-    return values * lax.rsqrt(jnp.mean(values * values, axis=-1, keepdims=True) + eps)
-
-
-def mix_kernel(
+    return multiply
+
+
+def layer_kernel(
     nz,
     nx,
-    p_ref,
+    x_ref,
+    pw_hbm,
     cw_ref,
     gain_ref,
     wo_ref,
     sel_ref,
     col_ref,
     row_ref,
-    m_ref,
-    wcol_ref,
+    o_ref,
+    buf_in,
+    pwv,
+    acc_in,
+    p_ref,
     halo,
     raw,
     cv,
@@ -216,25 +191,39 @@
     own,
     win,
     mine,
-    zbuf,
+    zin,
+    zpre,
+    zout,
     tot,
     xbuf,
-    pre,
+    prior,
     wcs,
+    mixed,
+    buf_out,
+    acc_out,
+    pwsem,
+    ssem_in,
+    rsem_in,
     hsem,
     zsend,
     zrecv,
     xsend,
     xrecv,
+    bsend,
+    brecv,
     wsend,
     wrecv,
     wloc,
+    ssem_out,
+    rsem_out,
 ):
     ctx = lax.axis_index("ctx")
     me = lax.axis_index("head")
     n_ctx = nz * nx
     n_head = 8
-    rows = p_ref.shape[0]
+    rows, depth = x_ref.shape
+    half = rows // 2
+    width = cw_ref.shape[1]
     per_head = 2 * FQK + 3 * DV
     out_rows = wo_ref.shape[0]
     out_cols = wo_ref.shape[1] // n_head
@@ -242,29 +231,34 @@
     z = lax.rem(ctx, nz)
     after, before = lax.rem(ctx + 1, n_ctx), lax.rem(ctx + n_ctx - 1, n_ctx)
 
-    def z_peer(d):
-        return (x * nz + lax.rem(z + d, nz), me)
-
-    def x_peer(d):
-        return (lax.rem(x + d, nx) * nz + z, me)
-
+    pw_copy = pltpu.make_async_copy(pw_hbm, pwv, pwsem)
+    pw_copy.start()
     barrier = pltpu.get_barrier_semaphore()
 
     def greet(dev):
         pl.semaphore_signal(barrier, inc=1, device_id=dev, device_id_type=MESH)
 
+    @pl.loop(1, nz)
+    def _(d):
+        greet((x * nz + lax.rem(z + d, nz), me))
+
     greet((after, me))
     greet((before, me))
-
-    @pl.loop(1, nz)
-    def _(d):
-        greet(z_peer(d))
-
     for d in range(1, nx):
-        greet(x_peer(d))
+        greet((lax.rem(x + d, nx) * nz + z, me))
     for d in range(1, n_head):
         greet((ctx, lax.rem(me + d, n_head)))
+
+    def project(part, owner):
+        return dot_nt(part, pwv[:, pl.ds(pl.multiple_of(owner * depth, depth), depth)])
+
+    multiply_in = make_multiply(acc_in, p_ref, half, project)
+    pw_copy.wait()
+    multiply_in(x_ref, me, 0, "first")
+    multiply_in(x_ref, me, 1, "first")
     pl.semaphore_wait(barrier, 2 + (nz - 1) + (nx - 1) + (n_head - 1))
+
+    sent = ring_gather(x_ref, buf_in, ctx, me, multiply_in, ssem_in, rsem_in, lambda: None)
 
     halo_copy = pltpu.make_async_remote_copy(
         src_ref=p_ref.at[pl.ds(rows - HALO, HALO)],
@@ -322,19 +316,25 @@
         lanes = slice(h * DV, (h + 1) * DV)
         mine[:, lanes] = dot(fk[h], cv[WIN:, lanes]).astype(BF16)
 
-    def z_copy(d):
+    def to_owner(s):
         return pltpu.make_async_remote_copy(
-            src_ref=mine,
-            dst_ref=zbuf.at[d],
-            send_sem=zsend.at[d],
-            recv_sem=zrecv.at[d],
-            device_id=z_peer(d),
+            src_ref=mine.at[pl.ds(s * SLICE, SLICE)],
+            dst_ref=zin.at[z],
+            send_sem=zsend.at[s],
+            recv_sem=zrecv.at[z],
+            device_id=(x * nz + OWNER_Z[s], me),
             device_id_type=MESH,
         )
 
-    @pl.loop(1, nz)
-    def _(d):
-        z_copy(d).start()
+    for s, z_owner in enumerate(OWNER_Z):
+
+        @pl.when(z != z_owner)
+        def _(s=s):
+            to_owner(s).start()
+
+        @pl.when(z == z_owner)
+        def _(s=s):
+            zin[z] = mine[s * SLICE : (s + 1) * SLICE, :]
 
     for h in range(2):
         base = h * per_head
@@ -387,17 +387,8 @@
 
     local_linear(0)
 
-    pre[...] = jnp.zeros_like(pre)
-    pre2 = mine[...].astype(F32)
-
-    def z_step(d, total):
-        z_copy(d).wait_recv()
-        part = zbuf[d].astype(F32)
-        pre[...] += jnp.where(d <= z, part, 0.0)
-        return total + part
-
-    plane = lax.fori_loop(1, nz, z_step, pre2)
-    tot[...] = plane.astype(BF16)
+    my_slice = lax.div(z * 5 + 7, 8)
+    is_owner = lax.div(my_slice * 8, 5) == z
 
     def x_copy(d):
         return pltpu.make_async_remote_copy(
@@ -405,12 +396,54 @@
             dst_ref=xbuf.at[d],
             send_sem=xsend.at[d],
             recv_sem=xrecv.at[d],
-            device_id=x_peer(d),
+            device_id=(lax.rem(x + d, nx) * nz + z, me),
             device_id_type=MESH,
         )
 
-    for d in range(1, nx):
-        x_copy(d).start()
+    def from_peer(peer):
+        return pltpu.make_async_remote_copy(
+            src_ref=mine.at[pl.ds(0, SLICE)],
+            dst_ref=zin.at[peer],
+            send_sem=zsend.at[0],
+            recv_sem=zrecv.at[peer],
+            device_id=(x * nz + peer, me),
+            device_id_type=MESH,
+        )
+
+    def back(peer):
+        return pltpu.make_async_remote_copy(
+            src_ref=zout.at[peer],
+            dst_ref=prior.at[pl.ds(pl.multiple_of(my_slice * SLICE, SLICE), SLICE)],
+            send_sem=bsend.at[peer],
+            recv_sem=brecv.at[my_slice],
+            device_id=(x * nz + peer, me),
+            device_id_type=MESH,
+        )
+
+    def back_from(s):
+        return pltpu.make_async_remote_copy(
+            src_ref=zout.at[0],
+            dst_ref=prior.at[pl.ds(s * SLICE, SLICE)],
+            send_sem=bsend.at[0],
+            recv_sem=brecv.at[s],
+            device_id=(x * nz + OWNER_Z[s], me),
+            device_id_type=MESH,
+        )
+
+    @pl.when(is_owner)
+    def _():
+        def scan(peer, run):
+            @pl.when(peer != z)
+            def _():
+                from_peer(peer).wait_recv()
+
+            zpre[peer] = run
+            return run + zin[peer].astype(F32)
+
+        plane = lax.fori_loop(0, nz, scan, jnp.zeros((SLICE, width), F32))
+        tot[...] = plane.astype(BF16)
+        for d in range(1, nx):
+            x_copy(d).start()
 
     for h in range(2):
         base = h * per_head
@@ -418,54 +451,103 @@
         a = dot_nt(query, sel_ref[0])
         b = dot_nt(query, sel_ref[1])
         fq[h] = (row_ref[0:1, :] * a * (b + row_ref[1:2, :]) + row_ref[2:3, :]).astype(BF16)
+
+    @pl.when(is_owner)
+    def _():
+        planes = jnp.zeros((SLICE, width), F32)
+        for d in range(1, nx):
+            x_copy(d).wait_recv()
+            planes += jnp.where(d <= x, xbuf[d].astype(F32), 0.0)
+
+        def answer(peer, planes):
+            value = (zpre[peer] + planes).astype(BF16)
+            zout[peer] = value
+
+            @pl.when(peer != z)
+            def _():
+                back(peer).start()
+
+            @pl.when(peer == z)
+            def _():
+                prior[pl.ds(pl.multiple_of(my_slice * SLICE, SLICE), SLICE), :] = value
+
+            return planes
+
+        lax.fori_loop(0, nz, answer, planes)
+
     local_linear(1)
 
-    for d in range(1, nx):
-        x_copy(d).wait_recv()
-        pre[...] += jnp.where(d <= x, xbuf[d].astype(F32), 0.0)
+    own_weight.wait()
+    for d in range(1, n_head):
+        weight_copy(d).wait_recv()
+    for s, z_owner in enumerate(OWNER_Z):
+
+        @pl.when(z != z_owner)
+        def _(s=s):
+            back_from(s).wait_recv()
 
     for h in range(2):
         lanes = slice(h * DV, (h + 1) * DV)
-        lin = own[:, lanes] + dot(fq[h], pre[:, lanes].astype(BF16))
+        lin = own[:, lanes] + dot(fq[h], prior[:, lanes])
         unit = rms_unit(lin, 1e-5)
-        m_ref[:, lanes] = (unit * gain_ref[:, lanes] + win[:, lanes]).astype(BF16)
-
-    own_weight.wait()
+        mixed[:, lanes] = (unit * gain_ref[:, lanes] + win[:, lanes]).astype(BF16)
+
+    def out_product(part, owner):
+        return dot(part, wcs[pl.ds(pl.multiple_of(owner * out_rows, out_rows), out_rows), :])
+
+    multiply_out = make_multiply(acc_out, o_ref, half, out_product)
+
+    def own_out():
+        multiply_out(mixed, me, 0, "first")
+        multiply_out(mixed, me, 1, "first")
+
+    sent += ring_gather(mixed, buf_out, ctx, me, multiply_out, ssem_out, rsem_out, own_out)
+
+    for copy in sent:
+        copy.wait_send()
     for d in range(1, n_head):
-        weight_copy(d).wait()
-    wcol_ref[...] = wcs[...]
-
-    @pl.loop(1, nz)
-    def _(d):
-        z_copy(d).wait_send()
-
-    for d in range(1, nx):
-        x_copy(d).wait_send()
+        weight_copy(d).wait_send()
+    for s, z_owner in enumerate(OWNER_Z):
+
+        @pl.when(z != z_owner)
+        def _(s=s):
+            to_owner(s).wait_send()
+
+    @pl.when(is_owner)
+    def _():
+        for d in range(1, nx):
+            x_copy(d).wait_send()
+
+        @pl.loop(0, nz)
+        def _(peer):
+            @pl.when(peer != z)
+            def _():
+                back(peer).wait_send()
 
 
 def per_device(hidden_in, proj_weight, conv_weight, norm_gain, out_weight):
-    rows = hidden_in.shape[0]
-    n_ctx = lax.axis_size("ctx")
+    rows, depth = hidden_in.shape
     nz = NZ
-    nx = n_ctx // nz
+    nx = lax.axis_size("ctx") // nz
     width = conv_weight.shape[1]
+    cols = proj_weight.shape[1]
     n_head = lax.axis_size("head")
     out_rows = out_weight.shape[0]
     out_cols = out_weight.shape[1] // n_head
     sel, coef = feature_tables()
-    projected = gather_matmul(hidden_in, proj_weight, "gather_project", 0)
     vmem = pl.BlockSpec(memory_space=pltpu.VMEM)
     dma = pltpu.SemaphoreType.DMA
-    mixed, out_cols_weight = pl.pallas_call(
-        functools.partial(mix_kernel, nz, nx),
-        out_shape=(
-            jax.ShapeDtypeStruct((rows, width), BF16),
-            jax.ShapeDtypeStruct((out_rows * n_head, out_cols), BF16),
-        ),
-        in_specs=[vmem] * 7,
-        out_specs=(vmem, vmem),
+    return pl.pallas_call(
+        functools.partial(layer_kernel, nz, nx),
+        out_shape=jax.ShapeDtypeStruct((rows, out_cols), BF16),
+        in_specs=[vmem, pl.BlockSpec(memory_space=pl.ANY)] + [vmem] * 6,
+        out_specs=vmem,
         scratch_shapes=[
-            pltpu.VMEM((HALO, projected.shape[1]), BF16),
+            pltpu.VMEM((7, rows, depth), BF16),
+            pltpu.VMEM((cols, depth * n_head), BF16),
+            pltpu.VMEM((rows, cols), F32),
+            pltpu.VMEM((rows, cols), BF16),
+            pltpu.VMEM((HALO, cols), BF16),
             pltpu.VMEM((rows + HALO, width), F32),
             pltpu.VMEM((rows + WIN, width), BF16),
             pltpu.VMEM((rows + WIN, width), BF16),
@@ -475,26 +557,39 @@
             pltpu.VMEM((rows, width), F32),
             pltpu.VMEM((rows, width), F32),
             pltpu.VMEM((FEAT, width), BF16),
-            pltpu.VMEM((nz, FEAT, width), BF16),
+            pltpu.VMEM((nz, SLICE, width), BF16),
+            pltpu.VMEM((nz, SLICE, width), F32),
+            pltpu.VMEM((nz, SLICE, width), BF16),
+            pltpu.VMEM((SLICE, width), BF16),
+            pltpu.VMEM((nx, SLICE, width), BF16),
             pltpu.VMEM((FEAT, width), BF16),
-            pltpu.VMEM((nx, FEAT, width), BF16),
-            pltpu.VMEM((FEAT, width), F32),
             pltpu.VMEM((out_rows * n_head, out_cols), BF16),
+            pltpu.VMEM((rows, width), BF16),
+            pltpu.VMEM((7, rows, width), BF16),
+            pltpu.VMEM((rows, out_cols), F32),
+            dma,
+            dma((14,)),
+            dma((14,)),
             dma((2,)),
-            dma((nz,)),
+            dma((len(OWNER_Z),)),
             dma((nz,)),
             dma((nx,)),
             dma((nx,)),
+            dma((nz,)),
+            dma((len(OWNER_Z),)),
             dma((n_head,)),
             dma((n_head,)),
             dma,
+            dma((14,)),
+            dma((14,)),
         ],
         compiler_params=pltpu.CompilerParams(
-            collective_id=1, has_side_effects=True, vmem_limit_bytes=56 << 20
+            collective_id=0, has_side_effects=True, vmem_limit_bytes=56 << 20
         ),
-        name="mix",
+        name="layer",
     )(
-        projected,
+        hidden_in,
+        proj_weight.T,
         conv_weight,
         norm_gain.reshape(1, width),
         out_weight,
@@ -502,7 +597,6 @@
         jnp.asarray(coef.T),
         jnp.asarray(coef),
     )
-    return gather_matmul(mixed, out_cols_weight, "gather_out", 2)
 
 
 def solution(mesh):

time: 109 us -> 82.9 us (0.76)
  Pallas kernels: 102 us -> 80.8 us
  local copies, waits for them, and re-layouts: 6.6 us -> 1.87 us
    pallas_call x3 -> x1, Pallas kernels: 102 us -> 80.8 us  [per_device(): pl.pallas_call(functools.partial(layer_kernel, nz, nx), out_shape=jax.Sha...]
    unnamed x10 -> x1, local copies, waits for them, and re-layouts: 6.6 us -> 1.87 us
where the time goes in v2:
time: 82.9 us; the launch traced here: 82.7 us
  Pallas kernels  80.8 us (97%)
  local copies, waits for them, and re-layouts  1.87 us (2%)
    pallas_call x1, Pallas kernels, per_device(): pl.pallas_call(functools.partial(layer_kernel, nz, nx), out_shape=jax.Sha...  80.8 us
    unnamed x1, local copies, waits for them, and re-layouts  1.87 us

profile of v2, /device:TPU:1, one launch (start us, length us, event | category | flops | bytes accessed | tf_op | source)
XLA Modules:
  0.0 82.7 jit_solution(10161833194107910255)
XLA Ops:
  0.0 80.8 %layer.1 = bf16[1024,256]{1,0:T(8,128)(2,1)} custom-call(bf16[1024,256]{1,0:T(8,128)(2,1)} %x_ref.1, bf16[448,2048]{1,0:T(8,128)(2,1)} %bitcast.2, f32[3,128]{1,0:T(4,128)} %cw_ref.1, f32[1,128]{1,0:T(1,128)} %bitcast.3, bf16[128,2048]{1,0:T(8,128)(2,1)} %wo_ref.1, bf16[2,160,16]{2,1,0:T(8,128)(2,1)} %constant.6.clone.sel_ref, ...), custom_call_target="tpu_custom_call" | custom-call | tf_op jit(solution)/shard_map/layer/pallas_call | solution.py:540
  80.9 1.9 %copy.10 = bf16[1024,256]{1,0:T(8,128)(2,1)} copy(bf16[1024,256]{1,0:T(8,128)(2,1)} %layer.1) | data formatting | bytes 1048576

commit v3 on v2

--- a/solution.py
+++ b/solution.py
@@ -17,6 +17,7 @@
 FEAT = 160
 SLICE = 16
 OWNER_Z = tuple(s * 8 // 5 for s in range(FEAT // SLICE))
+PARTS = 4
 MESH = pl.DeviceIdType.MESH
 F32 = jnp.float32
 BF16 = jnp.bfloat16
@@ -55,8 +56,8 @@
     return values * lax.rsqrt(jnp.mean(values * values, axis=-1, keepdims=True) + eps)
 
 
-def ring_gather(x_ref, buf, ctx, me, multiply, ssem, rsem, after_start):
-    half = x_ref.shape[0] // 2
+def ring_gather(x_ref, buf, ctx, me, multiply, ssem, rsem, ready, after_start):
+    size = x_ref.shape[0] // PARTS
     y = lax.div(me, 2)
     core = lax.rem(me, 2)
     other = 1 - core
@@ -75,12 +76,12 @@
     sent = []
 
     def send(src, slot, part, dev):
-        span = pl.ds(part * half, half)
+        span = pl.ds(part * size, size)
         copy = pltpu.make_async_remote_copy(
             src_ref=src.at[span],
             dst_ref=buf.at[slot, span],
             send_sem=ssem.at[len(sent)],
-            recv_sem=rsem.at[slot * 2 + part],
+            recv_sem=rsem.at[slot * PARTS + part],
             device_id=(ctx, dev),
             device_id_type=MESH,
         )
@@ -88,12 +89,12 @@
         sent.append(copy)
 
     def arrived(slot, part):
-        span = pl.ds(part * half, half)
+        span = pl.ds(part * size, size)
         pltpu.make_async_remote_copy(
             src_ref=buf.at[slot, span],
             dst_ref=buf.at[slot, span],
             send_sem=ssem.at[0],
-            recv_sem=rsem.at[slot * 2 + part],
+            recv_sem=rsem.at[slot * PARTS + part],
             device_id=(ctx, partner),
             device_id_type=MESH,
         ).wait_recv()
@@ -101,56 +102,70 @@
     def use(slot, part, mode="add"):
         multiply(buf.at[slot], owners[slot], part, mode)
 
-    send(x_ref, 0, 0, right)
-    send(x_ref, 1, 1, left)
-    send(x_ref, 3, 0, partner)
-    send(x_ref, 3, 1, partner)
-    send(x_ref, 0, 1, right)
-    send(x_ref, 1, 0, left)
+    lower = list(range(PARTS // 2))
+    upper = list(range(PARTS // 2, PARTS))
+    for part in lower:
+        ready(part)
+        send(x_ref, 0, part, right)
+    for part in upper:
+        ready(part)
+        send(x_ref, 1, part, left)
+    for part in upper:
+        send(x_ref, 0, part, right)
+    for part in lower:
+        send(x_ref, 1, part, left)
+    for part in lower + upper:
+        send(x_ref, 3, part, partner)
     after_start()
-    for part in (0, 1):
+    for part in lower + upper:
         arrived(3, part)
         use(3, part)
-    arrived(0, 0)
-    send(buf.at[0], 2, 0, right)
-    send(buf.at[0], 4, 0, partner)
-    arrived(1, 1)
-    send(buf.at[1], 2, 1, left)
-    send(buf.at[1], 5, 1, partner)
-    use(0, 0)
-    use(1, 1)
-    arrived(4, 0)
-    use(4, 0)
-    arrived(5, 1)
-    use(5, 1)
-    arrived(0, 1)
-    send(buf.at[0], 4, 1, partner)
-    arrived(1, 0)
-    send(buf.at[1], 5, 0, partner)
-    use(0, 1)
-    use(1, 0)
-    arrived(4, 1)
-    use(4, 1)
-    arrived(5, 0)
-    use(5, 0)
-    arrived(2, 0)
-    send(buf.at[2], 6, 0, partner)
-    arrived(2, 1)
-    send(buf.at[2], 6, 1, partner)
-    use(2, 1)
-    use(2, 0)
-    for part in (1, 0):
-        arrived(6, part)
-        use(6, part, "last")
+    for lo, up in zip(lower, upper):
+        arrived(0, lo)
+        send(buf.at[0], 2, lo, right)
+        send(buf.at[0], 4, lo, partner)
+        arrived(1, up)
+        send(buf.at[1], 2, up, left)
+        send(buf.at[1], 5, up, partner)
+        use(0, lo)
+        use(1, up)
+    for lo, up in zip(lower, upper):
+        arrived(4, lo)
+        use(4, lo)
+        arrived(5, up)
+        use(5, up)
+    for lo, up in zip(lower, upper):
+        arrived(0, up)
+        send(buf.at[0], 4, up, partner)
+        arrived(1, lo)
+        send(buf.at[1], 5, lo, partner)
+        use(0, up)
+        use(1, lo)
+    for lo, up in zip(lower, upper):
+        arrived(4, up)
+        use(4, up)
+        arrived(5, lo)
+        use(5, lo)
+    for lo, up in zip(lower, upper):
+        arrived(2, lo)
+        send(buf.at[2], 6, lo, partner)
+        arrived(2, up)
+        send(buf.at[2], 6, up, partner)
+        use(2, up)
+        use(2, lo)
+    for lo, up in zip(lower, upper):
+        for part in (up, lo):
+            arrived(6, part)
+            use(6, part, "last")
     return sent
 
 
-def make_multiply(acc, o_ref, half, product):
-    tile = min(256, half)
+def make_multiply(acc, o_ref, size, product):
+    tile = min(256, size)
 
     def multiply(src, owner, part, mode="add"):
         def step(i, carry):
-            span = pl.ds(pl.multiple_of(part * half + i * tile, tile), tile)
+            span = pl.ds(pl.multiple_of(part * size + i * tile, tile), tile)
             term = product(src[span, :], owner)
             if mode == "first":
                 acc[span, :] = term
@@ -160,7 +175,7 @@
                 acc[span, :] += term
             return carry
 
-        lax.fori_loop(0, half // tile, step, 0)
+        lax.fori_loop(0, size // tile, step, 0)
 
     return multiply
 
@@ -168,15 +183,22 @@
 def layer_kernel(
     nz,
     nx,
+    x_hbm,
+    pw_hbm,
+    cw_hbm,
+    gain_hbm,
+    wo_hbm,
+    sel_hbm,
+    col_hbm,
+    row_hbm,
+    o_ref,
     x_ref,
-    pw_hbm,
     cw_ref,
     gain_ref,
     wo_ref,
     sel_ref,
     col_ref,
     row_ref,
-    o_ref,
     buf_in,
     pwv,
     acc_in,
@@ -202,6 +224,7 @@
     buf_out,
     acc_out,
     pwsem,
+    insem,
     ssem_in,
     rsem_in,
     hsem,
@@ -222,7 +245,7 @@
     n_ctx = nz * nx
     n_head = 8
     rows, depth = x_ref.shape
-    half = rows // 2
+    size = rows // PARTS
     width = cw_ref.shape[1]
     per_head = 2 * FQK + 3 * DV
     out_rows = wo_ref.shape[0]
@@ -231,8 +254,6 @@
     z = lax.rem(ctx, nz)
     after, before = lax.rem(ctx + 1, n_ctx), lax.rem(ctx + n_ctx - 1, n_ctx)
 
-    pw_copy = pltpu.make_async_copy(pw_hbm, pwv, pwsem)
-    pw_copy.start()
     barrier = pltpu.get_barrier_semaphore()
 
     def greet(dev):
@@ -249,16 +270,27 @@
     for d in range(1, n_head):
         greet((ctx, lax.rem(me + d, n_head)))
 
+    x_copy_in = pltpu.make_async_copy(x_hbm, x_ref, insem.at[0])
+    x_copy_in.start()
+    pw_copy = pltpu.make_async_copy(pw_hbm, pwv, pwsem)
+    pw_copy.start()
+    late = [(cw_hbm, cw_ref), (gain_hbm, gain_ref), (wo_hbm, wo_ref)]
+    late += [(sel_hbm, sel_ref), (col_hbm, col_ref), (row_hbm, row_ref)]
+    late = [pltpu.make_async_copy(a, b, insem.at[k + 1]) for k, (a, b) in enumerate(late)]
+    for copy in late:
+        copy.start()
+    x_copy_in.wait()
+
     def project(part, owner):
         return dot_nt(part, pwv[:, pl.ds(pl.multiple_of(owner * depth, depth), depth)])
 
-    multiply_in = make_multiply(acc_in, p_ref, half, project)
+    multiply_in = make_multiply(acc_in, p_ref, size, project)
     pw_copy.wait()
-    multiply_in(x_ref, me, 0, "first")
-    multiply_in(x_ref, me, 1, "first")
+    for part in range(PARTS):
+        multiply_in(x_ref, me, part, "first")
     pl.semaphore_wait(barrier, 2 + (nz - 1) + (nx - 1) + (n_head - 1))
 
-    sent = ring_gather(x_ref, buf_in, ctx, me, multiply_in, ssem_in, rsem_in, lambda: None)
+    sent = ring_gather(x_ref, buf_in, ctx, me, multiply_in, ssem_in, rsem_in, lambda part: None, lambda: None)
 
     halo_copy = pltpu.make_async_remote_copy(
         src_ref=p_ref.at[pl.ds(rows - HALO, HALO)],
@@ -269,6 +301,8 @@
         device_id_type=MESH,
     )
     halo_copy.start()
+    for copy in late:
+        copy.wait()
 
     def weight_copy(d):
         dev = lax.rem(me + d, n_head)
@@ -300,21 +334,33 @@
         at = base + 2 * FQK
         raw[HALO:, lanes] = p_ref[:, at : at + DV].astype(F32)
 
+    lead = HALO - WIN
+    head_rows = 128
+
+    def convolve(first, count):
+        total = cw_ref[0:1, :] * raw[lead + first : lead + first + count, :]
+        for j in range(1, CONV):
+            at = lead + first - j
+            total = total + cw_ref[j : j + 1, :] * raw[at : at + count, :]
+        cv[first : first + count, :] = total.astype(BF16)
+
+    def state(first, count, h):
+        lanes = slice(h * DV, (h + 1) * DV)
+        return dot(
+            fk[h, :, first : first + count], cv[WIN + first : WIN + first + count, lanes]
+        )
+
+    convolve(WIN + head_rows, rows - head_rows)
+    main = [state(head_rows, rows - head_rows, h) for h in range(2)]
     halo_copy.wait()
     for h in range(2):
         at = h * per_head + 2 * FQK
         lanes = slice(h * DV, (h + 1) * DV)
         raw[:HALO, lanes] = jnp.where(ctx > 0, halo[:, at : at + DV].astype(F32), 0.0)
-    n_ext = rows + WIN
-    lead = HALO - WIN
-    total = cw_ref[0:1, :] * raw[lead : lead + n_ext, :]
-    for j in range(1, CONV):
-        total = total + cw_ref[j : j + 1, :] * raw[lead - j : lead - j + n_ext, :]
-    cv[...] = total.astype(BF16)
-
+    convolve(0, WIN + head_rows)
     for h in range(2):
         lanes = slice(h * DV, (h + 1) * DV)
-        mine[:, lanes] = dot(fk[h], cv[WIN:, lanes]).astype(BF16)
+        mine[:, lanes] = (main[h] + state(0, head_rows, h)).astype(BF16)
 
     def to_owner(s):
         return pltpu.make_async_remote_copy(
@@ -486,22 +532,24 @@
         def _(s=s):
             back_from(s).wait_recv()
 
-    for h in range(2):
-        lanes = slice(h * DV, (h + 1) * DV)
-        lin = own[:, lanes] + dot(fq[h], prior[:, lanes])
-        unit = rms_unit(lin, 1e-5)
-        mixed[:, lanes] = (unit * gain_ref[:, lanes] + win[:, lanes]).astype(BF16)
+    def mix_part(part):
+        span = slice(part * size, (part + 1) * size)
+        for h in range(2):
+            lanes = slice(h * DV, (h + 1) * DV)
+            lin = own[span, lanes] + dot(fq[h, span, :], prior[:, lanes])
+            unit = rms_unit(lin, 1e-5)
+            mixed[span, lanes] = (unit * gain_ref[:, lanes] + win[span, lanes]).astype(BF16)
 
     def out_product(part, owner):
         return dot(part, wcs[pl.ds(pl.multiple_of(owner * out_rows, out_rows), out_rows), :])
 
-    multiply_out = make_multiply(acc_out, o_ref, half, out_product)
+    multiply_out = make_multiply(acc_out, o_ref, size, out_product)
 
     def own_out():
-        multiply_out(mixed, me, 0, "first")
-        multiply_out(mixed, me, 1, "first")
-
-    sent += ring_gather(mixed, buf_out, ctx, me, multiply_out, ssem_out, rsem_out, own_out)
+        for part in range(PARTS):
+            multiply_out(mixed, me, part, "first")
+
+    sent += ring_gather(mixed, buf_out, ctx, me, multiply_out, ssem_out, rsem_out, mix_part, own_out)
 
     for copy in sent:
         copy.wait_send()
@@ -540,9 +588,16 @@
     return pl.pallas_call(
         functools.partial(layer_kernel, nz, nx),
         out_shape=jax.ShapeDtypeStruct((rows, out_cols), BF16),
-        in_specs=[vmem, pl.BlockSpec(memory_space=pl.ANY)] + [vmem] * 6,
+        in_specs=[pl.BlockSpec(memory_space=pltpu.HBM)] * 8,
         out_specs=vmem,
         scratch_shapes=[
+            pltpu.VMEM((rows, depth), BF16),
+            pltpu.VMEM(conv_weight.shape, F32),
+            pltpu.VMEM((1, width), F32),
+            pltpu.VMEM(out_weight.shape, BF16),
+            pltpu.VMEM(sel.shape, BF16),
+            pltpu.VMEM(coef.T.shape, F32),
+            pltpu.VMEM(coef.shape, F32),
             pltpu.VMEM((7, rows, depth), BF16),
             pltpu.VMEM((cols, depth * n_head), BF16),
             pltpu.VMEM((rows, cols), F32),
@@ -568,8 +623,9 @@
             pltpu.VMEM((7, rows, width), BF16),
             pltpu.VMEM((rows, out_cols), F32),
             dma,
-            dma((14,)),
-            dma((14,)),
+            dma((7,)),
+            dma((7 * PARTS,)),
+            dma((7 * PARTS,)),
             dma((2,)),
             dma((len(OWNER_Z),)),
             dma((nz,)),
@@ -580,11 +636,11 @@
             dma((n_head,)),
             dma((n_head,)),
             dma,
-            dma((14,)),
-            dma((14,)),
+            dma((7 * PARTS,)),
+            dma((7 * PARTS,)),
         ],
         compiler_params=pltpu.CompilerParams(
-            collective_id=0, has_side_effects=True, vmem_limit_bytes=56 << 20
+            collective_id=0, has_side_effects=True, vmem_limit_bytes=58000000
         ),
         name="layer",
     )(

time: 82.9 us -> 79.8 us (0.963)
  Pallas kernels: 80.8 us -> 77.7 us
    pallas_call x1, Pallas kernels: 80.8 us -> 77.7 us  [per_device(): pl.pallas_call(functools.partial(layer_kernel, nz, nx), out_shape=jax.Sha...]
where the time goes in v3:
time: 79.8 us; the launch traced here: 79.6 us
  Pallas kernels  77.7 us (97%)
  local copies, waits for them, and re-layouts  1.87 us (2%)
    pallas_call x1, Pallas kernels, per_device(): pl.pallas_call(functools.partial(layer_kernel, nz, nx), out_shape=jax.Sha...  77.7 us
    unnamed x1, local copies, waits for them, and re-layouts  1.87 us

profile of v3, /device:TPU:1, one launch (start us, length us, event | category | flops | bytes accessed | tf_op | source)
XLA Modules:
  0.0 79.6 jit_solution(795405911637150460)
XLA Ops:
  0.0 77.7 %layer.1 = bf16[1024,256]{1,0:T(8,128)(2,1)} custom-call(bf16[1024,256]{1,0:T(8,128)(2,1)} %x_hbm.1, bf16[448,2048]{1,0:T(8,128)(2,1)} %bitcast.2, f32[3,128]{1,0:T(4,128)} %cw_hbm.1, f32[1,128]{1,0:T(1,128)} %bitcast.3, bf16[128,2048]{1,0:T(8,128)(2,1)} %wo_hbm.1, bf16[2,160,16]{2,1,0:T(8,128)(2,1)} %constant.6.clone.sel_hbm, ...), custom_call_target="tpu_custom_call" | custom-call | tf_op jit(solution)/shard_map/layer/pallas_call | solution.py:588
  77.7 1.9 %copy.10 = bf16[1024,256]{1,0:T(8,128)(2,1)} copy(bf16[1024,256]{1,0:T(8,128)(2,1)} %layer.1) | data formatting | bytes 1048576

commit v4 on v3

--- a/solution.py
+++ b/solution.py
@@ -56,7 +56,7 @@
     return values * lax.rsqrt(jnp.mean(values * values, axis=-1, keepdims=True) + eps)
 
 
-def ring_gather(x_ref, buf, ctx, me, multiply, ssem, rsem, ready, after_start):
+def ring_gather(x_ref, buf, ctx, me, multiply, ssem, rsem, ready, after_start, tick):
     size = x_ref.shape[0] // PARTS
     y = lax.div(me, 2)
     core = lax.rem(me, 2)
@@ -129,11 +129,13 @@
         send(buf.at[1], 5, up, partner)
         use(0, lo)
         use(1, up)
+        tick()
     for lo, up in zip(lower, upper):
         arrived(4, lo)
         use(4, lo)
         arrived(5, up)
         use(5, up)
+        tick()
     for lo, up in zip(lower, upper):
         arrived(0, up)
         send(buf.at[0], 4, up, partner)
@@ -141,11 +143,13 @@
         send(buf.at[1], 5, lo, partner)
         use(0, up)
         use(1, lo)
+        tick()
     for lo, up in zip(lower, upper):
         arrived(4, up)
         use(4, up)
         arrived(5, lo)
         use(5, lo)
+        tick()
     for lo, up in zip(lower, upper):
         arrived(2, lo)
         send(buf.at[2], 6, lo, partner)
@@ -239,6 +243,7 @@
     wloc,
     ssem_out,
     rsem_out,
+    tokens,
 ):
     ctx = lax.axis_index("ctx")
     me = lax.axis_index("head")
@@ -259,10 +264,9 @@
     def greet(dev):
         pl.semaphore_signal(barrier, inc=1, device_id=dev, device_id_type=MESH)
 
-    @pl.loop(1, nz)
-    def _(d):
-        greet((x * nz + lax.rem(z + d, nz), me))
-
+    z_sides = ((x * nz + lax.rem(z + 1, nz), me), (x * nz + lax.rem(z + nz - 1, nz), me))
+    for dev in z_sides:
+        greet(dev)
     greet((after, me))
     greet((before, me))
     for d in range(1, nx):
@@ -288,9 +292,27 @@
     pw_copy.wait()
     for part in range(PARTS):
         multiply_in(x_ref, me, part, "first")
-    pl.semaphore_wait(barrier, 2 + (nz - 1) + (nx - 1) + (n_head - 1))
-
-    sent = ring_gather(x_ref, buf_in, ctx, me, multiply_in, ssem_in, rsem_in, lambda part: None, lambda: None)
+    pl.semaphore_wait(barrier, 2 + 2 + (nx - 1) + (n_head - 1))
+
+    rounds = nz // 2 - 1
+    passed = []
+
+    def tell():
+        for dev in z_sides:
+            pl.semaphore_signal(
+                tokens.at[len(passed)], inc=1, device_id=dev, device_id_type=MESH
+            )
+
+    def tick():
+        if len(passed) < rounds:
+            pl.semaphore_wait(tokens.at[len(passed)], 2)
+            passed.append(1)
+            if len(passed) < rounds:
+                tell()
+
+    tell()
+
+    sent = ring_gather(x_ref, buf_in, ctx, me, multiply_in, ssem_in, rsem_in, lambda part: None, lambda: None, tick)
 
     halo_copy = pltpu.make_async_remote_copy(
         src_ref=p_ref.at[pl.ds(rows - HALO, HALO)],
@@ -549,7 +571,7 @@
         for part in range(PARTS):
             multiply_out(mixed, me, part, "first")
 
-    sent += ring_gather(mixed, buf_out, ctx, me, multiply_out, ssem_out, rsem_out, mix_part, own_out)
+    sent += ring_gather(mixed, buf_out, ctx, me, multiply_out, ssem_out, rsem_out, mix_part, own_out, lambda: None)
 
     for copy in sent:
         copy.wait_send()
@@ -638,20 +660,26 @@
             dma,
             dma((7 * PARTS,)),
             dma((7 * PARTS,)),
+            pltpu.SemaphoreType.REGULAR((nz // 2 - 1,)),
         ],
         compiler_params=pltpu.CompilerParams(
-            collective_id=0, has_side_effects=True, vmem_limit_bytes=58000000
+            collective_id=0, has_side_effects=True, vmem_limit_bytes=48 << 20
         ),
         name="layer",
     )(
-        hidden_in,
-        proj_weight.T,
-        conv_weight,
-        norm_gain.reshape(1, width),
-        out_weight,
-        jnp.asarray(sel, BF16),
-        jnp.asarray(coef.T),
-        jnp.asarray(coef),
+        *(
+            pltpu.with_memory_space_constraint(value, pltpu.HBM)
+            for value in (
+                hidden_in,
+                proj_weight.T,
+                conv_weight,
+                norm_gain.reshape(1, width),
+                out_weight,
+                jnp.asarray(sel, BF16),
+                jnp.asarray(coef.T),
+                jnp.asarray(coef),
+            )
+        )
     )
 
 

time: 79.8 us -> 74.7 us (0.936)
  Pallas kernels: 77.7 us -> 73.7 us
  local copies, waits for them, and re-layouts: 1.87 us -> 0.8 us
    pallas_call x1, Pallas kernels: 77.7 us -> 73.7 us  [per_device(): pl.pallas_call(functools.partial(layer_kernel, nz, nx), out_shape=jax.Sha...]
    unnamed x1, local copies, waits for them, and re-layouts: 1.87 us -> 0.8 us
where the time goes in v4:
time: 74.7 us; the launch traced here: 74.5 us
  Pallas kernels  73.7 us (99%)
  local copies, waits for them, and re-layouts  0.8 us (1%)
    pallas_call x1, Pallas kernels, per_device(): pl.pallas_call(functools.partial(layer_kernel, nz, nx), out_shape=jax.Sha...  73.7 us

profile of v4, /device:TPU:1, one launch (start us, length us, event | category | flops | bytes accessed | tf_op | source)
XLA Modules:
  0.0 74.5 jit_solution(7921472302490117593)
XLA Ops:
  0.0 73.7 %layer.1 = bf16[1024,256]{1,0:T(8,128)(2,1)S(1)} custom-call(bf16[1024,256]{1,0:T(8,128)(2,1)} %x_hbm.1, bf16[448,2048]{1,0:T(8,128)(2,1)} %bitcast.2, f32[3,128]{1,0:T(4,128)} %cw_hbm.1, f32[1,128]{1,0:T(1,128)} %bitcast.3, bf16[128,2048]{1,0:T(8,128)(2,1)} %wo_hbm.1, bf16[2,160,16]{2,1,0:T(8,128)(2,1)} %constant.6.clone.sel_hbm, ...), custom_call_target="tpu_custom_call" | custom-call | tf_op jit(solution)/shard_map/layer/pallas_call | solution.py:610
  73.7 0.8 %copy.10 = bf16[1024,256]{1,0:T(8,128)(2,1)} copy(bf16[1024,256]{1,0:T(8,128)(2,1)S(1)} %layer.1) | data formatting | bytes 1048576

commit v5 on v4

--- a/solution.py
+++ b/solution.py
@@ -453,8 +453,6 @@
                 result = term if result is None else result + term
             own[i * qb : (i + 1) * qb, lanes] = result
 
-    local_linear(0)
-
     my_slice = lax.div(z * 5 + 7, 8)
     is_owner = lax.div(my_slice * 8, 5) == z
 
@@ -513,6 +511,29 @@
         for d in range(1, nx):
             x_copy(d).start()
 
+    @pl.when(is_owner)
+    def _():
+        planes = jnp.zeros((SLICE, width), F32)
+        for d in range(1, nx):
+            x_copy(d).wait_recv()
+            planes += jnp.where(d <= x, xbuf[d].astype(F32), 0.0)
+
+        def answer(peer, planes):
+            value = (zpre[peer] + planes).astype(BF16)
+            zout[peer] = value
+
+            @pl.when(peer != z)
+            def _():
+                back(peer).start()
+
+            @pl.when(peer == z)
+            def _():
+                prior[pl.ds(pl.multiple_of(my_slice * SLICE, SLICE), SLICE), :] = value
+
+            return planes
+
+        lax.fori_loop(0, nz, answer, planes)
+
     for h in range(2):
         base = h * per_head
         query = p_ref[:, base : base + FQK]
@@ -520,29 +541,7 @@
         b = dot_nt(query, sel_ref[1])
         fq[h] = (row_ref[0:1, :] * a * (b + row_ref[1:2, :]) + row_ref[2:3, :]).astype(BF16)
 
-    @pl.when(is_owner)
-    def _():
-        planes = jnp.zeros((SLICE, width), F32)
-        for d in range(1, nx):
-            x_copy(d).wait_recv()
-            planes += jnp.where(d <= x, xbuf[d].astype(F32), 0.0)
-
-        def answer(peer, planes):
-            value = (zpre[peer] + planes).astype(BF16)
-            zout[peer] = value
-
-            @pl.when(peer != z)
-            def _():
-                back(peer).start()
-
-            @pl.when(peer == z)
-            def _():
-                prior[pl.ds(pl.multiple_of(my_slice * SLICE, SLICE), SLICE), :] = value
-
-            return planes
-
-        lax.fori_loop(0, nz, answer, planes)
-
+    local_linear(0)
     local_linear(1)
 
     own_weight.wait()

time: 74.7 us -> 73.5 us (0.984)
  Pallas kernels: 73.7 us -> 72.6 us
    pallas_call x1, Pallas kernels: 73.7 us -> 72.6 us  [per_device(): pl.pallas_call(functools.partial(layer_kernel, nz, nx), out_shape=jax.Sha...]
where the time goes in v5:
time: 73.5 us; the launch traced here: 73.4 us
  Pallas kernels  72.6 us (99%)
  local copies, waits for them, and re-layouts  0.8 us (1%)
    pallas_call x1, Pallas kernels, per_device(): pl.pallas_call(functools.partial(layer_kernel, nz, nx), out_shape=jax.Sha...  72.6 us

profile of v5, /device:TPU:1, one launch (start us, length us, event | category | flops | bytes accessed | tf_op | source)
XLA Modules:
  0.0 73.4 jit_solution(11198907794092772825)
XLA Ops:
  0.0 72.6 %layer.1 = bf16[1024,256]{1,0:T(8,128)(2,1)S(1)} custom-call(bf16[1024,256]{1,0:T(8,128)(2,1)} %x_hbm.1, bf16[448,2048]{1,0:T(8,128)(2,1)} %bitcast.2, f32[3,128]{1,0:T(4,128)} %cw_hbm.1, f32[1,128]{1,0:T(1,128)} %bitcast.3, bf16[128,2048]{1,0:T(8,128)(2,1)} %wo_hbm.1, bf16[2,160,16]{2,1,0:T(8,128)(2,1)} %constant.6.clone.sel_hbm, ...), custom_call_target="tpu_custom_call" | custom-call | tf_op jit(solution)/shard_map/layer/pallas_call | solution.py:609
  72.6 0.8 %copy.10 = bf16[1024,256]{1,0:T(8,128)(2,1)} copy(bf16[1024,256]{1,0:T(8,128)(2,1)S(1)} %layer.1) | data formatting | bytes 1048576
